TPU v7x, 32 devices: a whole 2x2x4 slice. The times are simulated.
32 devices in a mesh: grp: 2 (over y), blk: 4 (over z), sub: 2 (over x), frq: 2 (over core).
Axes of the slice: x: 2, y: 2, z: 4, core: 2. Of those that a mesh axis runs over, the one named last changes fastest.
Arguments:
- spectra: bfloat16 [2, 8192, 4096], P(None, ('grp', 'blk'), ('sub', 'frq')), parts along dimension 1, may hold values from -6 to 6
- channel_mask: int32 [8, 1024], P(('grp', 'blk')), parts along dimension 0, may hold values 0 or 1
- local_channel: int32 [8, 4, 48], P(('grp', 'blk')), parts along dimension 0, may hold values from 0 to 1023
- partner_channel: int32 [8, 4, 48], P(('grp', 'blk')), parts along dimension 0, may hold values from 0 to 31
- stack_owner: int32 [8, 4, 48, 1], P(('grp', 'blk')), parts along dimension 0, may hold values from 0 to 3; in each aligned block of 192 rows (0 to 191, 192 to 383, ..., all dimensions but the last counted through in order) at most 96 rows name the same one
- stack_slot: int32 [8, 4, 48], P(('grp', 'blk')), parts along dimension 0, may hold values from 0 to 31
Outputs:
- stacks: float32 [256, 1024], P(('grp', 'blk'), ('sub', 'frq')), parts along dimension 0
There are 2 independent parts, one for each index of `grp`. A program takes and returns all parts, laid end to end along the dimension named above; each array names one. Nothing has to cross between parts.
Inputs may be any that keep to these rules, and one draw needn't show every extreme that they name: `stack_owner`: of the pairs of one source block, at most 96 name one owner, a bound that some block reaches of them.
All inputs are finite; a program needn't handle non-finite values. No bound on the sum of `channel_mask` on one device may be relied on, other than what follows from the above.
Results may differ from a plain program's by a relative error of at most 0.009.
Values may be sent and summed in bfloat16 or wider, within the bound.
A program may use at most 64 MiB of HBM per device.

v0:
```python
import math

import jax
import jax.numpy as jnp
from jax import lax
from jax.sharding import PartitionSpec as P

NF = 4096
LAGS = 1024
VS_BLK = 32
SLOTS_DEV = 32
CAP = 96


def from_root(block, axis, owner):
    block = jnp.where(lax.axis_index(axis) == owner, block, jnp.zeros_like(block))
    return lax.psum(block, axis)


def lag_rows(first_bin, bin_count):
    bin_index = first_bin + jnp.arange(bin_count, dtype=jnp.int32)
    shifts = jnp.arange(LAGS, dtype=jnp.int32) - LAGS // 2
    phase_angle = jnp.mod(bin_index[:, None] * shifts[None, :], NF).astype(jnp.float32) * (
        2.0 * math.pi / NF
    )
    factor = 1.0 / math.sqrt(NF)
    return jnp.concatenate(
        [jnp.cos(phase_angle) * factor, -jnp.sin(phase_angle) * factor], axis=0
    ).astype(jnp.bfloat16)


def per_device(spectra, channel_mask, local_channel, partner_channel, stack_owner, stack_slot):
    blocks = lax.axis_size("blk")
    bins_here = spectra.shape[2]
    lag_table = lag_rows(lax.axis_index(("sub", "frq")) * bins_here, bins_here)
    masked = spectra * channel_mask[0].astype(jnp.bfloat16)[None, :, None]
    stride_size = masked.shape[1] // VS_BLK
    own_panel = masked.reshape(2, VS_BLK, stride_size, bins_here)[:, :, 0, :]
    local_rows = local_channel[0]
    partner_rows = partner_channel[0]
    pair_step = local_rows.shape[1]
    empty_terms = jnp.zeros((blocks * pair_step, lag_table.shape[1]), jnp.float32)

    def add_pairs(partial_terms, panel_data, source):
        own_pick = lax.dynamic_index_in_dim(local_rows, source, 0, keepdims=False)
        partner_pick = lax.dynamic_index_in_dim(partner_rows, source, 0, keepdims=False)
        own_spectra = jnp.take(masked, own_pick, axis=1).astype(jnp.float32)
        partner_spectra = jnp.take(panel_data, partner_pick, axis=1).astype(jnp.float32)
        real_part = (
            own_spectra[0] * partner_spectra[0] + own_spectra[1] * partner_spectra[1]
        ).astype(jnp.bfloat16)
        imag_part = (
            own_spectra[1] * partner_spectra[0] - own_spectra[0] * partner_spectra[1]
        ).astype(jnp.bfloat16)
        cross_rows = jnp.concatenate([real_part, imag_part], axis=1)
        products = jnp.dot(cross_rows, lag_table, preferred_element_type=jnp.float32)
        start_row = (source * pair_step).astype(jnp.int32)
        return lax.dynamic_update_slice_in_dim(partial_terms, products, start_row, 0)

    def root_turn(turn_index, partial_terms):
        panel_data = from_root(own_panel, "blk", turn_index)
        return add_pairs(partial_terms, panel_data, turn_index)

    partial_terms = lax.fori_loop(0, blocks, root_turn, empty_terms)
    summed = lax.psum_scatter(
        partial_terms.astype(jnp.bfloat16), ("sub", "frq"), scatter_dimension=1, tiled=True
    )
    owners = stack_owner[0].reshape(-1)
    slots_flat = stack_slot[0].reshape(-1)
    lag_width = summed.shape[1]
    owner_hits = (owners[:, None] == jnp.arange(blocks, dtype=jnp.int32)[None, :]).astype(jnp.int32)
    earlier_hits = jnp.cumsum(owner_hits, axis=0) - owner_hits
    bucket_rank = jnp.sum(earlier_hits * owner_hits, axis=1)
    targets = owners * CAP + bucket_rank
    outgoing = jnp.zeros((blocks * CAP, lag_width), jnp.bfloat16).at[targets].set(summed)
    labels = (
        jnp.full((blocks * CAP,), -1.0, jnp.bfloat16)
        .at[targets]
        .set(slots_flat.astype(jnp.bfloat16))
    )
    arrived, arrived_labels = (
        lax.all_to_all(
            outgoing.reshape(blocks, CAP, lag_width), "blk", split_axis=0, concat_axis=0, tiled=True
        ),
        lax.all_to_all(labels.reshape(blocks, CAP), "blk", split_axis=0, concat_axis=0, tiled=True),
    )
    slot_ids = arrived_labels.reshape(-1).astype(jnp.int32)
    selector = (jnp.arange(SLOTS_DEV, dtype=jnp.int32)[:, None] == slot_ids[None, :]).astype(
        jnp.bfloat16
    )
    result_stacks = jnp.dot(
        selector, arrived.reshape(blocks * CAP, lag_width), preferred_element_type=jnp.float32
    )
    return result_stacks


def solution(mesh):
    return jax.shard_map(
        per_device,
        mesh=mesh,
        in_specs=(
            P(None, ("grp", "blk"), ("sub", "frq")),
            P(("grp", "blk"), None),
            P(("grp", "blk"), None, None),
            P(("grp", "blk"), None, None),
            P(("grp", "blk"), None, None, None),
            P(("grp", "blk"), None, None),
        ),
        out_specs=P(("grp", "blk"), ("sub", "frq")),
        check_vma=False,
    )
```

profile of v0, /device:TPU:0, one launch (start us, length us, event | category | flops | bytes accessed | tf_op | source)
XLA Modules:
  0.0 259.1 jit_solution(5674109913671485158)
XLA Ops:
  8.1 2.5 broadcast_multiply_fusion
  10.6 6.2 %copy.30 = bf16[2,1024,1024]{2,0,1:T(2,128)(2,1)} copy(bf16[2,1024,1024]{2,1,0:T(8,128)(2,1)S(1)} %broadcast_multiply_fusion) | data formatting | bytes 8388608 | tf_op jit(solution)/shard_map/while | solution.py:64
  17.3 17.6 %multiply_convert_fusion.1 = (bf16[1024,1024]{1,0:T(8,128)(2,1)S(1)}, bf16[1024,1024]{1,0:T(8,128)(2,1)S(1)}) fusion(s32[1024]{0:T(1024)S(1)} %get-tuple-element.182, s32[1024]{0:T(1024)S(1)} %get-tuple-element.183), kind=kLoop, calls=%fused_computation.40 | loop fusion | flops 19922944 | bytes 4202496 | tf_op jit(solution)/shard_map/convert.4
  34.9 2.4 pad_maximum_fusion
  37.4 176.2 %while.13 = (s32[]{:T(128)}, bf16[192,1024]{1,0:T(8,128)(2,1)S(1)}, s32[4,48]{1,0:T(4,128)S(1)}, bf16[2,1024,1024]{2,0,1:T(2,128)(2,1)}, s32[4,48]{1,0:T(4,128)S...) while((s32[]{:T(128)}, bf16[192,1024]{1,0:T(8,128)(2,1)S(1)}, ...), condition=%wide.region_6.7_spmd, body=%wide.region_4.6_spmd.sunk | while | flops 202640240 | bytes 8989001 | solution.py:64
  38.3 3.1 %gather_fusion.1 = bf16[48,2,1024]{2,1,0:T(2,128)(2,1)S(1)} fusion(bf16[2,1024,1024]{2,0,1:T(2,128)(2,1)} %get-tuple-element.268, s32[1024]{0:T(1024)S(1)} %pad_clamp_fusion.5), kind=kCustom, calls=%fused_computation.clone.1 | custom fusion | bytes 393408 | tf_op jit(solution)/shard_map/while/body/eval_jaxpr/jit(_take)/gather | solution.py:47
  41.7 36.2 %all-reduce.3.cloned.1.call-done = bf16[2,32,1024]{2,0,1:T(2,128)(2,1)} async-done(((bf16[2,32,1024]{2,0,1:T(2,128)(2,1)}), bf16[2,32,1024]{2,0,1:T(2,128)(2,1)}) %all-reduce.3.cloned.1.call-update) | async-done | bytes 131088 | tf_op jit(solution)/shard_map/while/body/eval_jaxpr/psum | solution.py:17
  77.9 1.9 gather_fusion
  80.7 3.0 %convolution_dynamic-update-slice_fusion.2 = bf16[192,1024]{1,0:T(8,128)(2,1)S(1)} fusion(bf16[192,1024]{1,0:T(8,128)(2,1)S(1)} %get-tuple-element.253, s32[]{:T(128)S(6)} %select_n.154, bf16[2048,1024]{1,0:T(8,128)(2,1)} %get-tuple-element.271, bf16[48,1024]{1,0:T(8,128)(2,1)S(1)} %bitcast.61, bf16[48,1024]{1,0:T(8,128)(2,1)S(1)} %bitcast.62), kind=kOutput, calls=%fused_computation.4.clone.1 | convolution fusion | flops 201719808 | bytes 4587524 | tf_op jit(solution)/shard_map/while/body/eval_jaxpr/dot_general | solution.py:56
  84.7 3.1 %gather_fusion.1 = bf16[48,2,1024]{2,1,0:T(2,128)(2,1)S(1)} fusion(bf16[2,1024,1024]{2,0,1:T(2,128)(2,1)} %get-tuple-element.268, s32[1024]{0:T(1024)S(1)} %pad_clamp_fusion.5), kind=kCustom, calls=%fused_computation.clone.1 | custom fusion | bytes 393408 | tf_op jit(solution)/shard_map/while/body/eval_jaxpr/jit(_take)/gather | solution.py:47
  88.1 33.2 %all-reduce.3.cloned.1.call-done = bf16[2,32,1024]{2,0,1:T(2,128)(2,1)} async-done(((bf16[2,32,1024]{2,0,1:T(2,128)(2,1)}), bf16[2,32,1024]{2,0,1:T(2,128)(2,1)}) %all-reduce.3.cloned.1.call-update) | async-done | bytes 131088 | tf_op jit(solution)/shard_map/while/body/eval_jaxpr/psum | solution.py:17
  124.1 3.0 %convolution_dynamic-update-slice_fusion.2 = bf16[192,1024]{1,0:T(8,128)(2,1)S(1)} fusion(bf16[192,1024]{1,0:T(8,128)(2,1)S(1)} %get-tuple-element.253, s32[]{:T(128)S(6)} %select_n.154, bf16[2048,1024]{1,0:T(8,128)(2,1)} %get-tuple-element.271, bf16[48,1024]{1,0:T(8,128)(2,1)S(1)} %bitcast.61, bf16[48,1024]{1,0:T(8,128)(2,1)S(1)} %bitcast.62), kind=kOutput, calls=%fused_computation.4.clone.1 | convolution fusion | flops 201719808 | bytes 4587524 | tf_op jit(solution)/shard_map/while/body/eval_jaxpr/dot_general | solution.py:56
  128.0 3.1 %gather_fusion.1 = bf16[48,2,1024]{2,1,0:T(2,128)(2,1)S(1)} fusion(bf16[2,1024,1024]{2,0,1:T(2,128)(2,1)} %get-tuple-element.268, s32[1024]{0:T(1024)S(1)} %pad_clamp_fusion.5), kind=kCustom, calls=%fused_computation.clone.1 | custom fusion | bytes 393408 | tf_op jit(solution)/shard_map/while/body/eval_jaxpr/jit(_take)/gather | solution.py:47
  131.5 33.2 %all-reduce.3.cloned.1.call-done = bf16[2,32,1024]{2,0,1:T(2,128)(2,1)} async-done(((bf16[2,32,1024]{2,0,1:T(2,128)(2,1)}), bf16[2,32,1024]{2,0,1:T(2,128)(2,1)}) %all-reduce.3.cloned.1.call-update) | async-done | bytes 131088 | tf_op jit(solution)/shard_map/while/body/eval_jaxpr/psum | solution.py:17
  164.7 1.9 gather_fusion
  167.5 3.0 %convolution_dynamic-update-slice_fusion.2 = bf16[192,1024]{1,0:T(8,128)(2,1)S(1)} fusion(bf16[192,1024]{1,0:T(8,128)(2,1)S(1)} %get-tuple-element.253, s32[]{:T(128)S(6)} %select_n.154, bf16[2048,1024]{1,0:T(8,128)(2,1)} %get-tuple-element.271, bf16[48,1024]{1,0:T(8,128)(2,1)S(1)} %bitcast.61, bf16[48,1024]{1,0:T(8,128)(2,1)S(1)} %bitcast.62), kind=kOutput, calls=%fused_computation.4.clone.1 | convolution fusion | flops 201719808 | bytes 4587524 | tf_op jit(solution)/shard_map/while/body/eval_jaxpr/dot_general | solution.py:56
  171.4 3.1 %gather_fusion.1 = bf16[48,2,1024]{2,1,0:T(2,128)(2,1)S(1)} fusion(bf16[2,1024,1024]{2,0,1:T(2,128)(2,1)} %get-tuple-element.268, s32[1024]{0:T(1024)S(1)} %pad_clamp_fusion.5), kind=kCustom, calls=%fused_computation.clone.1 | custom fusion | bytes 393408 | tf_op jit(solution)/shard_map/while/body/eval_jaxpr/jit(_take)/gather | solution.py:47
  174.8 32.9 %all-reduce.3.cloned.1.call-done = bf16[2,32,1024]{2,0,1:T(2,128)(2,1)} async-done(((bf16[2,32,1024]{2,0,1:T(2,128)(2,1)}), bf16[2,32,1024]{2,0,1:T(2,128)(2,1)}) %all-reduce.3.cloned.1.call-update) | async-done | bytes 131088 | tf_op jit(solution)/shard_map/while/body/eval_jaxpr/psum | solution.py:17
  210.5 3.0 %convolution_dynamic-update-slice_fusion.2 = bf16[192,1024]{1,0:T(8,128)(2,1)S(1)} fusion(bf16[192,1024]{1,0:T(8,128)(2,1)S(1)} %get-tuple-element.253, s32[]{:T(128)S(6)} %select_n.154, bf16[2048,1024]{1,0:T(8,128)(2,1)} %get-tuple-element.271, bf16[48,1024]{1,0:T(8,128)(2,1)S(1)} %bitcast.61, bf16[48,1024]{1,0:T(8,128)(2,1)S(1)} %bitcast.62), kind=kOutput, calls=%fused_computation.4.clone.1 | convolution fusion | flops 201719808 | bytes 4587524 | tf_op jit(solution)/shard_map/while/body/eval_jaxpr/dot_general | solution.py:56
  219.9 3.4 %all-to-all-start = ((bf16[4,1,96]{2,1,0:T(2,128)(2,1)}), bf16[4,1,96]{2,1,0:T(2,128)(2,1)S(1)}, u32[]{:S(2)}, u32[]{:S(2)}) async-start(bf16[4,1,96]{2,1,0:T(2,128)(2,1)} %all_to_all.12), calls=%async_computation | async-start | bytes 4096 | tf_op jit(solution)/shard_map/all_to_all | solution.py:85
  223.3 13.7 %reduce-scatter.2.cloned.1.call-done = bf16[192,256]{1,0:T(8,128)(2,1)} async-done(((bf16[192,1024]{1,0:T(8,128)(2,1)}), bf16[192,256]{1,0:T(8,128)(2,1)}) %reduce-scatter.2.cloned.1.call-update) | async-done | bytes 98320 | tf_op jit(solution)/shard_map/reduce_scatter | solution.py:65
  237.0 2.2 scatter_custom_fusion.1
  239.3 4.6 %all-to-all-start.1 = ((bf16[4,96,256]{2,1,0:T(8,128)(2,1)}), bf16[4,96,256]{2,1,0:T(8,128)(2,1)S(1)}, u32[]{:S(2)}, u32[]{:S(2)}) async-start(bf16[4,96,256]{2,1,0:T(8,128)(2,1)} %bitcast.16), calls=%async_computation.2 | async-start | bytes 393216 | tf_op jit(solution)/shard_map/all_to_all | solution.py:82
  244.0 7.2 %all-to-all-done.1 = bf16[4,96,256]{2,1,0:T(8,128)(2,1)S(1)} async-done(((bf16[4,96,256]{2,1,0:T(8,128)(2,1)}), bf16[4,96,256]{2,1,0:T(8,128)(2,1)S(1)}, u32[]{:S(2)}, u32[]{:S(2)}) %all-to-all-start.1) | async-done | bytes 196640 | tf_op jit(solution)/shard_map/all_to_all | solution.py:82
  (92 shorter events, 20.1 us)
Async XLA Ops:
  34.8 2.5 copy-start.1
  34.8 2.5 copy-start.2
  37.3 177.5 %copy-start.4 = (s32[1,4,48,1]{2,3,1,0:T(1,128)S(1)}, s32[1,4,48,1]{2,3,1,0:T(1,128)}, u32[]{:S(2)}) copy-start(s32[1,4,48,1]{2,3,1,0:T(1,128)} %param.12) | copy-start | bytes 2308
  37.3 180.0 %copy-start.3 = (s32[1,4,48]{2,1,0:T(4,128)S(1)}, s32[1,4,48]{2,1,0:T(4,128)}, u32[]{:S(2)}) copy-start(s32[1,4,48]{2,1,0:T(4,128)} %param.13) | copy-start | bytes 2308
  37.4 40.5 %all-reduce.3.cloned.1.call-start = ((), (), s32[]{:S(2)}) async-start(), calls=%async_computation.4 | async-start | bytes 262144 | tf_op jit(solution)/shard_map/while/body/eval_jaxpr/psum | solution.py:17
  83.8 37.5 %all-reduce.3.cloned.1.call-start = ((), (), s32[]{:S(2)}) async-start(), calls=%async_computation.4 | async-start | bytes 262144 | tf_op jit(solution)/shard_map/while/body/eval_jaxpr/psum | solution.py:17
  127.2 37.5 %all-reduce.3.cloned.1.call-start = ((), (), s32[]{:S(2)}) async-start(), calls=%async_computation.4 | async-start | bytes 262144 | tf_op jit(solution)/shard_map/while/body/eval_jaxpr/psum | solution.py:17
  170.5 37.2 %all-reduce.3.cloned.1.call-start = ((), (), s32[]{:S(2)}) async-start(), calls=%async_computation.4 | async-start | bytes 262144 | tf_op jit(solution)/shard_map/while/body/eval_jaxpr/psum | solution.py:17
  213.6 0.7 copy-start
  213.6 23.4 %reduce-scatter.2.cloned.1.call-start = ((), (), s32[]{:S(2)}) async-start(), calls=%async_computation.3 | async-start | bytes 491520 | tf_op jit(solution)/shard_map/reduce_scatter | solution.py:65
  219.9 19.4 %all-to-all-start = ((bf16[4,1,96]{2,1,0:T(2,128)(2,1)}), bf16[4,1,96]{2,1,0:T(2,128)(2,1)S(1)}, u32[]{:S(2)}, u32[]{:S(2)}) async-start(bf16[4,1,96]{2,1,0:T(2,128)(2,1)} %all_to_all.12), calls=%async_computation | async-start | bytes 4096 | tf_op jit(solution)/shard_map/all_to_all | solution.py:85
  239.3 11.9 %all-to-all-start.1 = ((bf16[4,96,256]{2,1,0:T(8,128)(2,1)}), bf16[4,96,256]{2,1,0:T(8,128)(2,1)S(1)}, u32[]{:S(2)}, u32[]{:S(2)}) async-start(bf16[4,96,256]{2,1,0:T(8,128)(2,1)} %bitcast.16), calls=%async_computation.2 | async-start | bytes 393216 | tf_op jit(solution)/shard_map/all_to_all | solution.py:82
Sparse Core Ops, SparseCore 0:
  40.5 37.3 all-reduce.2
  86.9 34.3 all-reduce.2
  130.3 34.3 all-reduce.2
  173.3 34.3 all-reduce.2
Sparse Core Ops, SparseCore 1:
  216.6 20.4 reduce-scatter.1
where the time goes:
time: 260 us; the launch traced here: 259 us
  waiting for transfers between devices  156 us (60%)
  local copies, waits for them, and re-layouts  33.3 us (13%)
  other arithmetic  32.9 us (13%)
  between operations  14.7 us (6%)
  matrix products  12.9 us (5%)
  starting transfers between devices  8.39 us (3%)
    psum x4, waiting for transfers between devices, from_root(): return lax.psum(block, axis)  135 us
    another operation x4, other arithmetic  18.8 us
    reduce_scatter x1, waiting for transfers between devices, per_device(): lax.psum_scatter(partial_terms.astype(jnp.bfloat16), ('sub', 'frq'), scat...  13.7 us
    gather x4, local copies, waits for them, and re-layouts, add_pairs(): own_spectra = jnp.take(masked, own_pick, axis=1).astype(jnp.float32)  12.6 us
    dot_general x4, matrix products, add_pairs(): jnp.dot(cross_rows, lag_table, preferred_element_type=jnp.float32)  12.1 us
    gather x4, local copies, waits for them, and re-layouts, add_pairs(): jnp.take(panel_data, partner_pick, axis=1).astype(jnp.float32)  7.43 us
    all_to_all x1, waiting for transfers between devices, per_device(): lax.all_to_all(outgoing.reshape(blocks, CAP, lag_width), 'blk', split_axi...  7.19 us
    while x2, local copies, waits for them, and re-layouts, per_device(): partial_terms = lax.fori_loop(0, blocks, root_turn, empty_terms)  6.44 us
  transfers between devices with their start and end apart: 7, of which 6 were waited for; matrix products, arithmetic and copies ran while one was open for 8% of the time, Pallas kernels for 0%

commit v1 on v0

v1 whole, which is shorter than its diff:
```python
import functools
import math

import jax
import jax.numpy as jnp
import numpy as np
from jax import lax
from jax.experimental import pallas as pl
from jax.experimental.pallas import tpu as pltpu
from jax.sharding import PartitionSpec as P

NF = 4096
LAGS = 1024
VS_BLK = 32
SLOTS_DEV = 32
STEP = 32
MESH = pl.DeviceIdType.MESH


def phase_rows(bins):
    shifts = np.arange(LAGS, dtype=np.int64) - LAGS // 2
    angle = np.mod(bins[:, None] * shifts[None, :], NF) * (2.0 * math.pi / NF)
    return np.stack([np.cos(angle), -np.sin(angle)])


def loop(count, body):
    if count == 1:
        body(0)
    else:
        lax.fori_loop(0, count, lambda i, carry: (body(i), carry)[1], 0)


def kernel(n, nsub, nfrq, chunks, pair_block, stack_block,
           spectra, mask_ref, cols_ref, rows_ref, coarse, fine_ref, out_ref,
           spec, tiles, panels, own, hot, sel, cross, stacked, table, coarse_v, acc,
           send1, recv1, total, send2, recv2,
           load_sem, right_send, right_recv, left_send, left_recv,
           s1_send, s1_recv, s2_send, s2_recv):
    z = lax.axis_index("blk")
    sub, frq = lax.axis_index("sub"), lax.axis_index("frq")
    place = sub * nfrq + frq
    channels, bins = spec.shape[1], spec.shape[2]
    width = bins // chunks
    pairs, stacks = own.shape[1], acc.shape[0]
    lag_width = out_ref.shape[1]
    coarse_rows = bins // STEP
    peers = [(ds, df) for ds in range(nsub - 1, -1, -1) for df in range(nfrq - 1, -1, -1)]

    tile_load = pltpu.make_async_copy(spectra.at[:, :, pl.ds(0, 8), :], tiles, load_sem.at[0])
    tile_load.start()
    flat = spectra.reshape(2, channels, bins)
    spec_loads = []
    for c in range(chunks):
        lanes = pl.ds(c * width, width)
        spec_loads.append(pltpu.make_async_copy(
            flat.at[:, :, lanes], spec.at[:, :, lanes], load_sem.at[2 + c]))
    coarse_load = pltpu.make_async_copy(
        coarse.at[:, pl.ds(pl.multiple_of(place * coarse_rows, 8), coarse_rows), :],
        coarse_v, load_sem.at[1])
    for load in spec_loads:
        load.start()
    coarse_load.start()

    barrier = pltpu.get_barrier_semaphore()
    for k in range(1, n):
        pl.semaphore_signal(barrier, inc=1, device_id={"blk": lax.rem(z + k, n)}, device_id_type=MESH)
    for ds, df in peers[:-1]:
        pl.semaphore_signal(
            barrier, inc=1,
            device_id={"sub": lax.rem(sub + ds, nsub), "frq": lax.rem(frq + df, nfrq)},
            device_id_type=MESH)

    mask = mask_ref[...]
    at_row = lax.broadcasted_iota(jnp.int32, (VS_BLK, channels), 0)
    at_lane = lax.broadcasted_iota(jnp.int32, (VS_BLK, channels), 1)
    source_mask = jnp.sum(
        jnp.where(at_lane == at_row * (channels // VS_BLK), mask, 0).astype(jnp.float32),
        axis=1, keepdims=True)
    pick_row = lax.broadcasted_iota(jnp.int32, (VS_BLK, 8 * VS_BLK), 0)
    pick_lane = lax.broadcasted_iota(jnp.int32, (VS_BLK, 8 * VS_BLK), 1)
    pick = jnp.where(pick_lane == 8 * pick_row, source_mask, 0.0).astype(jnp.bfloat16)
    tile_load.wait()
    for part in range(2):
        picked = jnp.dot(pick, tiles[part].reshape(8 * VS_BLK, bins),
                         preferred_element_type=jnp.float32).astype(jnp.bfloat16)
        for c in range(chunks):
            panels[z, c, part] = picked[:, c * width:(c + 1) * width]
    pl.semaphore_wait(barrier, n - 1 + len(peers) - 1)

    def to_right(c, d):
        return pltpu.make_async_remote_copy(
            src_ref=panels.at[z - d, c], dst_ref=panels.at[z - d, c],
            send_sem=right_send.at[c, d], recv_sem=right_recv.at[c, d],
            device_id={"blk": z + 1}, device_id_type=MESH)

    def to_left(c, d):
        return pltpu.make_async_remote_copy(
            src_ref=panels.at[z + d, c], dst_ref=panels.at[z + d, c],
            send_sem=left_send.at[c, d], recv_sem=left_recv.at[c, d],
            device_id={"blk": z - 1}, device_id_type=MESH)

    def from_left(c, d):
        return pltpu.make_async_remote_copy(
            src_ref=panels.at[z - 1 - d, c], dst_ref=panels.at[z - 1 - d, c],
            send_sem=right_send.at[c, d], recv_sem=right_recv.at[c, d],
            device_id={"blk": z - 1}, device_id_type=MESH)

    def from_right(c, d):
        return pltpu.make_async_remote_copy(
            src_ref=panels.at[z + 1 + d, c], dst_ref=panels.at[z + 1 + d, c],
            send_sem=left_send.at[c, d], recv_sem=left_recv.at[c, d],
            device_id={"blk": z + 1}, device_id_type=MESH)

    def send_on(c, d):
        @pl.when((z - d >= 0) & (z + 1 < n))
        def _():
            to_right(c, d).start()

        @pl.when((z + d < n) & (z - 1 >= 0))
        def _():
            to_left(c, d).start()

    def arrive(c, d):
        @pl.when(z - 1 - d >= 0)
        def _():
            from_left(c, d).wait_recv()

        @pl.when(z + 1 + d < n)
        def _():
            from_right(c, d).wait_recv()

        if d + 1 < n - 1:
            send_on(c, d + 1)

    for c in range(chunks):
        send_on(c, 0)

    def build_hot():
        def body(r):
            rows = pl.ds(pl.multiple_of(r * pair_block, 16), pair_block)
            lane = lax.broadcasted_iota(jnp.int32, (pair_block, channels), 1)
            hit = jnp.where(lane == cols_ref[rows, 0:1], mask, 0)
            hot[rows, :] = hit.astype(jnp.float32).astype(jnp.bfloat16)
        loop(pairs // pair_block, body)

        def body_sel(r):
            rows = pl.ds(pl.multiple_of(r * stack_block, 16), stack_block)
            row = lax.broadcasted_iota(jnp.int32, (stack_block, pairs), 0) + r * stack_block
            hit = jnp.where(row == rows_ref[0:1, :], 1.0, 0.0)
            sel[rows, :] = hit.astype(jnp.bfloat16)
        loop(stacks // stack_block, body_sel)

    def gather(c):
        spec_loads[c].wait()
        for part in range(2):
            def body(r):
                rows = pl.ds(pl.multiple_of(r * pair_block, 16), pair_block)
                lanes = pl.ds(c * width, width)
                own[part, rows, lanes] = jnp.dot(
                    hot[rows, :], spec[part, :, lanes],
                    preferred_element_type=jnp.float32).astype(jnp.bfloat16)
            loop(pairs // pair_block, body)

    def make_table(c):
        if c == 0:
            coarse_load.wait()

        def body(a):
            row = pl.ds(c * (width // STEP) + a, 1)
            high_cos, high_sin = coarse_v[0, row, :], coarse_v[1, row, :]
            low_cos, low_sin = fine_ref[0], fine_ref[1]
            rows = pl.ds(pl.multiple_of(a * STEP, STEP), STEP)
            table[c, 0, rows, :] = (high_cos * low_cos - high_sin * low_sin).astype(jnp.bfloat16)
            table[c, 1, rows, :] = (high_sin * low_cos + high_cos * low_sin).astype(jnp.bfloat16)
        loop(width // STEP, body)

    work = [functools.partial(build_hot)]
    for c in range(chunks):
        work += [functools.partial(gather, c), functools.partial(make_table, c)]
    work.pop(0)()
    work.pop(0)()

    for d in range(n - 2):
        for c in range(chunks):
            arrive(c, d)
            if work:
                work.pop(0)()
    while work:
        work.pop(0)()

    def stack_chunk(c):
        lanes = pl.ds(c * width, width)
        panel = [panels[:, c, part].reshape(n * VS_BLK, width) for part in range(2)]

        def body(r):
            rows = pl.ds(pl.multiple_of(r * pair_block, 16), pair_block)
            lane = lax.broadcasted_iota(jnp.int32, (pair_block, n * VS_BLK), 1)
            hit = jnp.where(lane == cols_ref[rows, 1:2], 1.0, 0.0).astype(jnp.bfloat16)
            partner = [jnp.dot(hit, half, preferred_element_type=jnp.float32) for half in panel]
            mine = [own[part, rows, lanes].astype(jnp.float32) for part in range(2)]
            cross[rows, 0:width] = (
                mine[0] * partner[0] + mine[1] * partner[1]).astype(jnp.bfloat16)
            cross[rows, width:2 * width] = (
                mine[1] * partner[0] - mine[0] * partner[1]).astype(jnp.bfloat16)
        loop(pairs // pair_block, body)

        def body_stack(r):
            rows = pl.ds(pl.multiple_of(r * stack_block, 16), stack_block)
            stacked[rows, :] = jnp.dot(
                sel[rows, :], cross[...], preferred_element_type=jnp.float32).astype(jnp.bfloat16)
        loop(stacks // stack_block, body_stack)

    for c in range(chunks):
        arrive(c, n - 2)
        stack_chunk(c)
        if c < chunks - 1:
            def body(r):
                rows = pl.ds(pl.multiple_of(r * stack_block, 16), stack_block)
                product = jnp.dot(
                    stacked[rows, :], table[c].reshape(2 * width, LAGS),
                    preferred_element_type=jnp.float32)
                acc[rows, :] = product if c == 0 else acc[rows, :] + product
            loop(stacks // stack_block, body)

    sends1 = []
    last = chunks - 1
    for k, (ds, df) in enumerate(peers):
        to_sub, to_frq = lax.rem(sub + ds, nsub), lax.rem(frq + df, nfrq)
        lanes = pl.ds(pl.multiple_of((to_sub * nfrq + to_frq) * lag_width, 128), lag_width)
        own_share = k == len(peers) - 1

        def body(r):
            rows = pl.ds(pl.multiple_of(r * stack_block, 16), stack_block)
            product = jnp.dot(
                stacked[rows, :], table[last, :, :, lanes].reshape(2 * width, lag_width),
                preferred_element_type=jnp.float32)
            if last > 0:
                product = product + acc[rows, lanes]
            if own_share:
                total[rows, :] = product
            else:
                send1[k, rows, :] = product.astype(jnp.bfloat16)
        loop(stacks // stack_block, body)
        if not own_share:
            copy = pltpu.make_async_remote_copy(
                src_ref=send1.at[k], dst_ref=recv1.at[k],
                send_sem=s1_send.at[k], recv_sem=s1_recv.at[k],
                device_id={"sub": to_sub, "frq": to_frq}, device_id_type=MESH)
            copy.start()
            sends1.append(copy)

    for copy in sends1:
        copy.wait_recv()
    summed = total[...]
    for k in range(len(peers) - 1):
        summed = summed + recv1[k].astype(jnp.float32)
    total[...] = summed
    send2[...] = summed.astype(jnp.bfloat16).reshape(n, SLOTS_DEV, lag_width)
    sends2 = []
    for k in range(n - 1, 0, -1):
        owner = lax.rem(z + k, n)
        copy = pltpu.make_async_remote_copy(
            src_ref=send2.at[owner], dst_ref=recv2.at[k - 1],
            send_sem=s2_send.at[k - 1], recv_sem=s2_recv.at[k - 1],
            device_id={"blk": owner}, device_id_type=MESH)
        copy.start()
        sends2.append(copy)
    result = total[pl.ds(pl.multiple_of(z * SLOTS_DEV, SLOTS_DEV), SLOTS_DEV), :]

    for c in range(chunks):
        for d in range(n - 1):
            @pl.when((z - d >= 0) & (z + 1 < n))
            def _():
                to_right(c, d).wait_send()

            @pl.when((z + d < n) & (z - 1 >= 0))
            def _():
                to_left(c, d).wait_send()
    for copy in sends1:
        copy.wait_send()
    for copy in sends2:
        copy.wait_recv()
    for k in range(n - 1):
        result = result + recv2[k].astype(jnp.float32)
    out_ref[...] = result
    for copy in sends2:
        copy.wait_send()


def per_device(sizes, spectra, channel_mask, local_channel, partner_channel, stack_owner, stack_slot):
    n, nsub, nfrq = sizes
    channels, bins = spectra.shape[1], spectra.shape[2]
    chunks = 4 if n <= 8 else 1
    width = bins // chunks
    pairs = local_channel.shape[1] * local_channel.shape[2]
    stacks = n * SLOTS_DEV
    lag_width = LAGS // (nsub * nfrq)
    pair_block = 192 if pairs % 192 == 0 else pairs
    stack_block = 128 if stacks % 128 == 0 else stacks
    panel_row = partner_channel[0] + (jnp.arange(n, dtype=jnp.int32) * VS_BLK)[:, None]
    cols = jnp.stack([local_channel[0].reshape(-1), panel_row.reshape(-1)], axis=1)
    rows = (stack_owner[0, :, :, 0] * SLOTS_DEV + stack_slot[0]).reshape(1, -1)
    coarse = (phase_rows(np.arange(0, NF, STEP)) / math.sqrt(NF)).astype(np.float32)
    fine = phase_rows(np.arange(STEP)).astype(np.float32)
    bf16, f32 = jnp.bfloat16, jnp.float32
    vmem = pl.BlockSpec(memory_space=pltpu.VMEM)
    hbm = pl.BlockSpec(memory_space=pl.ANY)
    peers = nsub * nfrq
    dma = pltpu.SemaphoreType.DMA
    return pl.pallas_call(
        functools.partial(kernel, n, nsub, nfrq, chunks, pair_block, stack_block),
        out_shape=jax.ShapeDtypeStruct((SLOTS_DEV, lag_width), f32),
        in_specs=[hbm, vmem, vmem, vmem, hbm, vmem],
        out_specs=vmem,
        scratch_shapes=[
            pltpu.VMEM((2, channels, bins), bf16),
            pltpu.VMEM((2, VS_BLK, 8, bins), bf16),
            pltpu.VMEM((n, chunks, 2, VS_BLK, width), bf16),
            pltpu.VMEM((2, pairs, bins), bf16),
            pltpu.VMEM((pairs, channels), bf16),
            pltpu.VMEM((stacks, pairs), bf16),
            pltpu.VMEM((pairs, 2 * width), bf16),
            pltpu.VMEM((stacks, 2 * width), bf16),
            pltpu.VMEM((chunks, 2, width, LAGS), bf16),
            pltpu.VMEM((2, bins // STEP, LAGS), f32),
            pltpu.VMEM((stacks, LAGS), f32),
            pltpu.VMEM((peers - 1, stacks, lag_width), bf16),
            pltpu.VMEM((peers - 1, stacks, lag_width), bf16),
            pltpu.VMEM((stacks, lag_width), f32),
            pltpu.VMEM((n, SLOTS_DEV, lag_width), bf16),
            pltpu.VMEM((n - 1, SLOTS_DEV, lag_width), bf16),
            dma((2 + chunks,)),
            dma((chunks, n - 1)), dma((chunks, n - 1)),
            dma((chunks, n - 1)), dma((chunks, n - 1)),
            dma((peers - 1,)), dma((peers - 1,)),
            dma((n - 1,)), dma((n - 1,)),
        ],
        compiler_params=pltpu.CompilerParams(collective_id=0, has_side_effects=True),
    )(spectra.reshape(2, VS_BLK, channels // VS_BLK, bins), channel_mask, cols, rows,
      jnp.asarray(coarse), jnp.asarray(fine))


def solution(mesh):
    sizes = (mesh.shape["blk"], mesh.shape["sub"], mesh.shape["frq"])
    return jax.shard_map(
        functools.partial(per_device, sizes),
        mesh=mesh,
        in_specs=(
            P(None, ("grp", "blk"), ("sub", "frq")),
            P(("grp", "blk"), None),
            P(("grp", "blk"), None, None),
            P(("grp", "blk"), None, None),
            P(("grp", "blk"), None, None, None),
            P(("grp", "blk"), None, None),
        ),
        out_specs=P(("grp", "blk"), ("sub", "frq")),
        check_vma=False,
    )
```

time: 260 us -> 33.3 us (0.13)
  waiting for transfers between devices: 156 us -> 0 us
  other arithmetic: 32.9 us -> 1.29 us
  local copies, waits for them, and re-layouts: 33.3 us -> 4.65 us
  Pallas kernels: 0 us -> 27.1 us
  between operations: 14.7 us -> 0.02 us
  matrix products: 12.9 us -> 0 us
  starting transfers between devices: 8.39 us -> 0 us
    psum x4 -> x0, waiting for transfers between devices: 135 us -> none  [from_root(): return lax.psum(block, axis)]
    pallas_call x0 -> x1, Pallas kernels: none -> 27.1 us  [per_device(): pl.pallas_call(functools.partial(kernel, n, nsub, nfrq, chunks, pair_bloc...]
    gather x8 -> x0, local copies, waits for them, and re-layouts: 20 us -> none  [the longest x4 12.6 us: add_pairs(): own_spectra = jnp.take(masked, own_pick, axis=1).astype(jnp.float32)]
    another operation x4 -> x1, other arithmetic: 18.8 us -> 0.01 us  [per_device(): jnp.stack([local_channel[0].reshape(-1), panel_row.reshape(-1)], axis=1)]
    reduce_scatter x1 -> x0, waiting for transfers between devices: 13.7 us -> none  [per_device(): lax.psum_scatter(partial_terms.astype(jnp.bfloat16), ('sub', 'frq'), scat...]
    dot_general x5 -> x0, matrix products: 12.9 us -> none  [the longest x4 12.1 us: add_pairs(): jnp.dot(cross_rows, lag_table, preferred_element_type=jnp.float32)]
    all_to_all x2 -> x0, starting transfers between devices: 8 us -> none  [the longest x1 4.6 us: per_device(): lax.all_to_all(outgoing.reshape(blocks, CAP, lag_width), 'blk', split_axi...]
    all_to_all x2 -> x0, waiting for transfers between devices: 7.2 us -> none  [the longest x1 7.19 us: per_device(): lax.all_to_all(outgoing.reshape(blocks, CAP, lag_width), 'blk', split_axi...]
  transfers between devices with their start and end apart: 7 -> 0, of which waited for: 6 -> 0; matrix products, arithmetic and copies ran while one was open for 8% -> 0% of each run, Pallas kernels for 0% -> 0%
where the time goes in v1:
time: 33.3 us; the launch traced here: 33 us
  Pallas kernels  27.1 us (81%)
  local copies, waits for them, and re-layouts  4.65 us (14%)
  other arithmetic  1.29 us (4%)
    pallas_call x1, Pallas kernels, per_device(): pl.pallas_call(functools.partial(kernel, n, nsub, nfrq, chunks, pair_bloc...  27.1 us
    another operation x2, local copies, waits for them, and re-layouts, per_device(): jnp.stack([local_channel[0].reshape(-1), panel_row.reshape(-1)], axis=1)  1.51 us
    unnamed x1, local copies, waits for them, and re-layouts  1.38 us
    squeeze x1, local copies, waits for them, and re-layouts, per_device(): partner_channel[0] + (jnp.arange(n, dtype=jnp.int32) * VS_BLK)[:, None]  0.76 us
    squeeze x1, local copies, waits for them, and re-layouts, per_device(): rows = (stack_owner[0, :, :, 0] * SLOTS_DEV + stack_slot[0]).reshape(1, -1)  0.76 us
    mul x1, other arithmetic, per_device(): rows = (stack_owner[0, :, :, 0] * SLOTS_DEV + stack_slot[0]).reshape(1, -1)  0.7 us

profile of v1, /device:TPU:0, one launch (start us, length us, event | category | flops | bytes accessed | tf_op | source)
XLA Modules:
  0.0 33.0 jit_solution(1438136879914686385)
XLA Ops:
  0.0 0.8 %stack_reshape_squeeze.3 = s32[192,1]{0,1:T(1,128)S(1)} reshape(s32[1,4,48]{2,1,0:T(4,128)} %param.10) | data formatting | bytes 1536 | tf_op jit(solution)/shard_map/stack;reshape;squeeze | solution.py:301
  0.8 0.8 %squeeze.7 = s32[192,1]{0,1:T(1,128)S(1)} reshape(s32[1,4,48]{2,1,0:T(4,128)} %param.11) | data formatting | bytes 1536 | tf_op jit(solution)/shard_map/squeeze | solution.py:300
  1.5 0.8 %squeeze.8 = s32[1,192]{1,0:T(1,128)S(1)} reshape(s32[1,4,48]{2,1,0:T(4,128)} %param.13) | data formatting | bytes 1536 | tf_op jit(solution)/shard_map/squeeze | solution.py:302
  2.3 0.1 add.27
  2.4 0.1 add.28
  2.5 0.7 %multiply_reduce_fusion = s32[4,48]{1,0:T(4,128)S(1)} fusion(s32[1,4,48,1]{2,3,1,0:T(1,128)} %param.12), kind=kLoop, calls=%fused_computation.1 | loop fusion | flops 192 | bytes 1536 | tf_op jit(solution)/shard_map/mul | solution.py:302
  3.2 0.1 mul.26
  3.3 0.6 %add.30.rows_ref = s32[1,192]{1,0:T(1,128)} add(s32[1,192]{1,0:T(1,128)S(1)} %mul.26, s32[1,192]{1,0:T(1,128)S(1)} %squeeze.8) | non-fusion elementwise | flops 192 | bytes 2304 | tf_op jit(solution)/shard_map/add | solution.py:302
  3.8 0.7 %copy.12.cols_ref = s32[192,2]{1,0:T(8,128)} copy(s32[192,2]{0,1:T(2,128)S(1)} %pad_add_fusion) | data formatting | bytes 3072 | tf_op jit(solution)/shard_map/stack | solution.py:301
  4.6 27.1 %shard_map.82 = f32[32,256]{1,0:T(8,128)} custom-call(bf16[2,32,32,1024]{3,2,1,0:T(8,128)(2,1)} %bitcast.1, s32[1,1024]{1,0:T(1,128)} %mask_ref.1, s32[192,2]{1,0:T(8,128)} %copy.12.cols_ref, s32[1,192]{1,0:T(1,128)} %add.30.rows_ref, f32[2,128,1024]{2,1,0:T(8,128)} %constant.2.clone.coarse, f32[2,32,1024]{2,1,0:T(8,128)} %constant.8.clone.fine_ref), custom_call_target="tpu_custom_call" | custom-call | tf_op jit(solution)/shard_map/pallas_call | solution.py:310
  31.6 1.4 %copy.14 = f32[32,256]{1,0:T(8,128)} copy(f32[32,256]{1,0:T(8,128)} %shard_map.82) | data formatting | bytes 65536
  (3 shorter events, 0.0 us)

commit v2 on v1

--- a/solution.py
+++ b/solution.py
@@ -31,7 +31,8 @@
 
 
 def kernel(n, nsub, nfrq, chunks, pair_block, stack_block,
-           spectra, mask_ref, cols_ref, rows_ref, coarse, fine_ref, out_ref,
+           spectra, mask_ref, local_ref, partner_ref, owner_ref, slot_ref, coarse, fine_ref, out_ref,
+           index_rows, index_cols, stack_row,
            spec, tiles, panels, own, hot, sel, cross, stacked, table, coarse_v, acc,
            send1, recv1, total, send2, recv2,
            load_sem, right_send, right_recv, left_send, left_recv,
@@ -136,17 +137,29 @@
         send_on(c, 0)
 
     def build_hot():
+        per_panel = local_ref.shape[2]
+        index_rows[...] = jnp.zeros_like(index_rows)
+        index_rows[0:n, 0:per_panel] = local_ref[0].astype(jnp.float32)
+        index_rows[n:2 * n, 0:per_panel] = partner_ref[0].astype(jnp.float32)
+        turned = index_rows[...].T
+        for p in range(n):
+            rows = pl.ds(p * per_panel, per_panel)
+            index_cols[rows, 0:1] = turned[0:per_panel, p:p + 1].astype(jnp.int32)
+            index_cols[rows, 1:2] = turned[0:per_panel, n + p:n + p + 1].astype(jnp.int32) + p * VS_BLK
+            stack_row[0:1, p * per_panel:(p + 1) * per_panel] = (
+                owner_ref[p] * SLOTS_DEV + slot_ref[0, p:p + 1, :])
+
         def body(r):
             rows = pl.ds(pl.multiple_of(r * pair_block, 16), pair_block)
             lane = lax.broadcasted_iota(jnp.int32, (pair_block, channels), 1)
-            hit = jnp.where(lane == cols_ref[rows, 0:1], mask, 0)
+            hit = jnp.where(lane == index_cols[rows, 0:1], mask, 0)
             hot[rows, :] = hit.astype(jnp.float32).astype(jnp.bfloat16)
         loop(pairs // pair_block, body)
 
         def body_sel(r):
             rows = pl.ds(pl.multiple_of(r * stack_block, 16), stack_block)
             row = lax.broadcasted_iota(jnp.int32, (stack_block, pairs), 0) + r * stack_block
-            hit = jnp.where(row == rows_ref[0:1, :], 1.0, 0.0)
+            hit = jnp.where(row == stack_row[0:1, :], 1.0, 0.0)
             sel[rows, :] = hit.astype(jnp.bfloat16)
         loop(stacks // stack_block, body_sel)
 
@@ -195,7 +208,7 @@
         def body(r):
             rows = pl.ds(pl.multiple_of(r * pair_block, 16), pair_block)
             lane = lax.broadcasted_iota(jnp.int32, (pair_block, n * VS_BLK), 1)
-            hit = jnp.where(lane == cols_ref[rows, 1:2], 1.0, 0.0).astype(jnp.bfloat16)
+            hit = jnp.where(lane == index_cols[rows, 1:2], 1.0, 0.0).astype(jnp.bfloat16)
             partner = [jnp.dot(hit, half, preferred_element_type=jnp.float32) for half in panel]
             mine = [own[part, rows, lanes].astype(jnp.float32) for part in range(2)]
             cross[rows, 0:width] = (
@@ -297,9 +310,6 @@
     lag_width = LAGS // (nsub * nfrq)
     pair_block = 192 if pairs % 192 == 0 else pairs
     stack_block = 128 if stacks % 128 == 0 else stacks
-    panel_row = partner_channel[0] + (jnp.arange(n, dtype=jnp.int32) * VS_BLK)[:, None]
-    cols = jnp.stack([local_channel[0].reshape(-1), panel_row.reshape(-1)], axis=1)
-    rows = (stack_owner[0, :, :, 0] * SLOTS_DEV + stack_slot[0]).reshape(1, -1)
     coarse = (phase_rows(np.arange(0, NF, STEP)) / math.sqrt(NF)).astype(np.float32)
     fine = phase_rows(np.arange(STEP)).astype(np.float32)
     bf16, f32 = jnp.bfloat16, jnp.float32
@@ -310,9 +320,12 @@
     return pl.pallas_call(
         functools.partial(kernel, n, nsub, nfrq, chunks, pair_block, stack_block),
         out_shape=jax.ShapeDtypeStruct((SLOTS_DEV, lag_width), f32),
-        in_specs=[hbm, vmem, vmem, vmem, hbm, vmem],
+        in_specs=[hbm, vmem, vmem, vmem, vmem, vmem, hbm, vmem],
         out_specs=vmem,
         scratch_shapes=[
+            pltpu.VMEM((128, 128), f32),
+            pltpu.VMEM((pairs, 2), jnp.int32),
+            pltpu.VMEM((1, pairs), jnp.int32),
             pltpu.VMEM((2, channels, bins), bf16),
             pltpu.VMEM((2, VS_BLK, 8, bins), bf16),
             pltpu.VMEM((n, chunks, 2, VS_BLK, width), bf16),
@@ -336,7 +349,8 @@
             dma((n - 1,)), dma((n - 1,)),
         ],
         compiler_params=pltpu.CompilerParams(collective_id=0, has_side_effects=True),
-    )(spectra.reshape(2, VS_BLK, channels // VS_BLK, bins), channel_mask, cols, rows,
+    )(spectra.reshape(2, VS_BLK, channels // VS_BLK, bins), channel_mask,
+      local_channel, partner_channel, stack_owner.reshape(n, 1, -1), stack_slot,
       jnp.asarray(coarse), jnp.asarray(fine))
 
 

time: 33.3 us -> 28.6 us (0.86)
  local copies, waits for them, and re-layouts: 4.65 us -> 1.38 us
  other arithmetic: 1.29 us -> 0 us
    squeeze x2 -> x0, local copies, waits for them, and re-layouts: 1.53 us -> none  [the longest x1 0.76 us: per_device(): partner_channel[0] + (jnp.arange(n, dtype=jnp.int32) * VS_BLK)[:, None]]
    another operation x2 -> x0, local copies, waits for them, and re-layouts: 1.51 us -> none  [per_device(): jnp.stack([local_channel[0].reshape(-1), panel_row.reshape(-1)], axis=1)]
    mul x2 -> x0, other arithmetic: 0.71 us -> none  [the longest x1 0.7 us: per_device(): rows = (stack_owner[0, :, :, 0] * SLOTS_DEV + stack_slot[0]).reshape(1, -1)]
    add x2 -> x0, other arithmetic: 0.58 us -> none  [the longest x1 0.57 us: per_device(): rows = (stack_owner[0, :, :, 0] * SLOTS_DEV + stack_slot[0]).reshape(1, -1)]
where the time goes in v2:
time: 28.6 us; the launch traced here: 28.4 us
  Pallas kernels  27 us (94%)
  local copies, waits for them, and re-layouts  1.38 us (5%)
    pallas_call x1, Pallas kernels, per_device(): pl.pallas_call(functools.partial(kernel, n, nsub, nfrq, chunks, pair_bloc...  27 us
    unnamed x1, local copies, waits for them, and re-layouts  1.38 us

profile of v2, /device:TPU:0, one launch (start us, length us, event | category | flops | bytes accessed | tf_op | source)
XLA Modules:
  0.0 28.4 jit_solution(11508858428063223366)
XLA Ops:
  0.0 27.0 %shard_map.82 = f32[32,256]{1,0:T(8,128)} custom-call(bf16[2,32,32,1024]{3,2,1,0:T(8,128)(2,1)} %bitcast.2, s32[1,1024]{1,0:T(1,128)} %mask_ref.1, s32[1,4,48]{2,1,0:T(4,128)} %local_ref.1, s32[1,4,48]{2,1,0:T(4,128)} %partner_ref.1, s32[4,1,48]{2,1,0:T(1,128)} %bitcast.3, s32[1,4,48]{2,1,0:T(4,128)} %slot_ref.1, f32[2,128,1024]{2,1,0:T(8,128)} %constant.4.clone.coarse, ...), custom_call_target="tpu_custom_call" | custom-call | tf_op jit(solution)/shard_map/pallas_call | solution.py:320
  27.1 1.4 %copy.10 = f32[32,256]{1,0:T(8,128)} copy(f32[32,256]{1,0:T(8,128)} %shard_map.82) | data formatting | bytes 65536

commit v3 on v2

--- a/solution.py
+++ b/solution.py
@@ -30,12 +30,20 @@
         lax.fori_loop(0, count, lambda i, carry: (body(i), carry)[1], 0)
 
 
+def steps(count, body):
+    if count <= 8:
+        for i in range(count):
+            body(i)
+    else:
+        lax.fori_loop(0, count, lambda i, carry: (body(i), carry)[1], 0)
+
+
 def kernel(n, nsub, nfrq, chunks, pair_block, stack_block,
            spectra, mask_ref, local_ref, partner_ref, owner_ref, slot_ref, coarse, fine_ref, out_ref,
            index_rows, index_cols, stack_row,
            spec, tiles, panels, own, hot, sel, cross, stacked, table, coarse_v, acc,
            send1, recv1, total, send2, recv2,
-           load_sem, right_send, right_recv, left_send, left_recv,
+           tile_sem, load_sem, right_send, right_recv, left_send, left_recv,
            s1_send, s1_recv, s2_send, s2_recv):
     z = lax.axis_index("blk")
     sub, frq = lax.axis_index("sub"), lax.axis_index("frq")
@@ -47,24 +55,32 @@
     coarse_rows = bins // STEP
     peers = [(ds, df) for ds in range(nsub - 1, -1, -1) for df in range(nfrq - 1, -1, -1)]
 
-    tile_load = pltpu.make_async_copy(spectra.at[:, :, pl.ds(0, 8), :], tiles, load_sem.at[0])
-    tile_load.start()
+    tile_loads = []
+    for c in range(chunks):
+        lanes = pl.ds(c * width, width)
+        tile_loads.append(pltpu.make_async_copy(
+            spectra.at[:, :, pl.ds(0, 8), lanes], tiles.at[:, :, :, lanes], tile_sem.at[c]))
+    for load in tile_loads:
+        load.start()
     flat = spectra.reshape(2, channels, bins)
     spec_loads = []
     for c in range(chunks):
         lanes = pl.ds(c * width, width)
         spec_loads.append(pltpu.make_async_copy(
-            flat.at[:, :, lanes], spec.at[:, :, lanes], load_sem.at[2 + c]))
+            flat.at[:, :, lanes], spec.at[:, :, lanes], load_sem.at[1 + c]))
     coarse_load = pltpu.make_async_copy(
         coarse.at[:, pl.ds(pl.multiple_of(place * coarse_rows, 8), coarse_rows), :],
-        coarse_v, load_sem.at[1])
-    for load in spec_loads:
-        load.start()
-    coarse_load.start()
-
+        coarse_v, load_sem.at[0])
     barrier = pltpu.get_barrier_semaphore()
-    for k in range(1, n):
-        pl.semaphore_signal(barrier, inc=1, device_id={"blk": lax.rem(z + k, n)}, device_id_type=MESH)
+
+    @pl.when(z + 1 < n)
+    def _():
+        pl.semaphore_signal(barrier, inc=1, device_id={"blk": z + 1}, device_id_type=MESH)
+
+    @pl.when(z - 1 >= 0)
+    def _():
+        pl.semaphore_signal(barrier, inc=1, device_id={"blk": z - 1}, device_id_type=MESH)
+
     for ds, df in peers[:-1]:
         pl.semaphore_signal(
             barrier, inc=1,
@@ -80,14 +96,6 @@
     pick_row = lax.broadcasted_iota(jnp.int32, (VS_BLK, 8 * VS_BLK), 0)
     pick_lane = lax.broadcasted_iota(jnp.int32, (VS_BLK, 8 * VS_BLK), 1)
     pick = jnp.where(pick_lane == 8 * pick_row, source_mask, 0.0).astype(jnp.bfloat16)
-    tile_load.wait()
-    for part in range(2):
-        picked = jnp.dot(pick, tiles[part].reshape(8 * VS_BLK, bins),
-                         preferred_element_type=jnp.float32).astype(jnp.bfloat16)
-        for c in range(chunks):
-            panels[z, c, part] = picked[:, c * width:(c + 1) * width]
-    pl.semaphore_wait(barrier, n - 1 + len(peers) - 1)
-
     def to_right(c, d):
         return pltpu.make_async_remote_copy(
             src_ref=panels.at[z - d, c], dst_ref=panels.at[z - d, c],
@@ -134,7 +142,19 @@
             send_on(c, d + 1)
 
     for c in range(chunks):
+        tile_loads[c].wait()
+        lanes = pl.ds(c * width, width)
+        for part in range(2):
+            panels[z, c, part] = jnp.dot(
+                pick, tiles[part, :, :, lanes].reshape(8 * VS_BLK, width),
+                preferred_element_type=jnp.float32).astype(jnp.bfloat16)
+        if c == 0:
+            ends = jnp.where(z == 0, 1, 0) + jnp.where(z == n - 1, 1, 0)
+            pl.semaphore_wait(barrier, len(peers) + 1 - ends)
         send_on(c, 0)
+    for load in spec_loads:
+        load.start()
+    coarse_load.start()
 
     def build_hot():
         per_panel = local_ref.shape[2]
@@ -235,8 +255,31 @@
                 acc[rows, :] = product if c == 0 else acc[rows, :] + product
             loop(stacks // stack_block, body)
 
-    sends1 = []
+    targets = []
     last = chunks - 1
+
+    def owner_at(j):
+        return jnp.where(z < n // 2, n - 1 - j, j)
+
+    def share_copy(k, owner):
+        rows = pl.ds(pl.multiple_of(owner * SLOTS_DEV, SLOTS_DEV), SLOTS_DEV)
+        return pltpu.make_async_remote_copy(
+            src_ref=send1.at[k, rows, :], dst_ref=recv1.at[k, rows, :],
+            send_sem=s1_send.at[k, owner], recv_sem=s1_recv.at[k, owner],
+            device_id={"sub": targets[k][0], "frq": targets[k][1]}, device_id_type=MESH)
+
+    def owner_copy(owner):
+        return pltpu.make_async_remote_copy(
+            src_ref=send2.at[owner], dst_ref=recv2.at[z],
+            send_sem=s2_send.at[owner], recv_sem=s2_recv.at[z],
+            device_id={"blk": owner}, device_id_type=MESH)
+
+    def send_shares(ks):
+        def turn(j):
+            for k in ks:
+                share_copy(k, owner_at(j)).start()
+        steps(n, turn)
+
     for k, (ds, df) in enumerate(peers):
         to_sub, to_frq = lax.rem(sub + ds, nsub), lax.rem(frq + df, nfrq)
         lanes = pl.ds(pl.multiple_of((to_sub * nfrq + to_frq) * lag_width, 128), lag_width)
@@ -254,30 +297,26 @@
             else:
                 send1[k, rows, :] = product.astype(jnp.bfloat16)
         loop(stacks // stack_block, body)
-        if not own_share:
-            copy = pltpu.make_async_remote_copy(
-                src_ref=send1.at[k], dst_ref=recv1.at[k],
-                send_sem=s1_send.at[k], recv_sem=s1_recv.at[k],
-                device_id={"sub": to_sub, "frq": to_frq}, device_id_type=MESH)
-            copy.start()
-            sends1.append(copy)
-
-    for copy in sends1:
-        copy.wait_recv()
-    summed = total[...]
-    for k in range(len(peers) - 1):
-        summed = summed + recv1[k].astype(jnp.float32)
-    total[...] = summed
-    send2[...] = summed.astype(jnp.bfloat16).reshape(n, SLOTS_DEV, lag_width)
-    sends2 = []
-    for k in range(n - 1, 0, -1):
-        owner = lax.rem(z + k, n)
-        copy = pltpu.make_async_remote_copy(
-            src_ref=send2.at[owner], dst_ref=recv2.at[k - 1],
-            send_sem=s2_send.at[k - 1], recv_sem=s2_recv.at[k - 1],
-            device_id={"blk": owner}, device_id_type=MESH)
-        copy.start()
-        sends2.append(copy)
+        targets.append((to_sub, to_frq))
+        if k == max(len(peers) - 3, 0):
+            send_shares(range(k + 1))
+        elif not own_share and k > len(peers) - 3:
+            send_shares([k])
+
+    def owner_turn(j):
+        owner = owner_at(j)
+        rows = pl.ds(pl.multiple_of(owner * SLOTS_DEV, SLOTS_DEV), SLOTS_DEV)
+        summed = total[rows, :]
+        for k in range(len(peers) - 1):
+            share_copy(k, owner).wait_recv()
+            summed = summed + recv1[k, rows, :].astype(jnp.float32)
+        total[rows, :] = summed
+        send2[owner] = summed.astype(jnp.bfloat16)
+
+        @pl.when(owner != z)
+        def _():
+            owner_copy(owner).start()
+    steps(n, owner_turn)
     result = total[pl.ds(pl.multiple_of(z * SLOTS_DEV, SLOTS_DEV), SLOTS_DEV), :]
 
     for c in range(chunks):
@@ -289,15 +328,21 @@
             @pl.when((z + d < n) & (z - 1 >= 0))
             def _():
                 to_left(c, d).wait_send()
-    for copy in sends1:
-        copy.wait_send()
-    for copy in sends2:
-        copy.wait_recv()
-    for k in range(n - 1):
-        result = result + recv2[k].astype(jnp.float32)
+    def shares_left(j):
+        for k in range(len(peers) - 1):
+            share_copy(k, j).wait_send()
+    steps(n, shares_left)
     out_ref[...] = result
-    for copy in sends2:
-        copy.wait_send()
+
+    def add_block(k):
+        source = lax.rem(z + 1 + k, n)
+        pltpu.make_async_remote_copy(
+            src_ref=send2.at[source], dst_ref=recv2.at[source],
+            send_sem=s2_send.at[source], recv_sem=s2_recv.at[source],
+            device_id={"blk": source}, device_id_type=MESH).wait_recv()
+        out_ref[...] += recv2[source].astype(jnp.float32)
+    steps(n - 1, add_block)
+    steps(n - 1, lambda k: owner_copy(lax.rem(z + 1 + k, n)).wait_send())
 
 
 def per_device(sizes, spectra, channel_mask, local_channel, partner_channel, stack_owner, stack_slot):
@@ -341,12 +386,12 @@
             pltpu.VMEM((peers - 1, stacks, lag_width), bf16),
             pltpu.VMEM((stacks, lag_width), f32),
             pltpu.VMEM((n, SLOTS_DEV, lag_width), bf16),
-            pltpu.VMEM((n - 1, SLOTS_DEV, lag_width), bf16),
-            dma((2 + chunks,)),
+            pltpu.VMEM((n, SLOTS_DEV, lag_width), bf16),
+            dma((chunks,)), dma((1 + chunks,)),
             dma((chunks, n - 1)), dma((chunks, n - 1)),
             dma((chunks, n - 1)), dma((chunks, n - 1)),
-            dma((peers - 1,)), dma((peers - 1,)),
-            dma((n - 1,)), dma((n - 1,)),
+            dma((peers - 1, n)), dma((peers - 1, n)),
+            dma((n,)), dma((n,)),
         ],
         compiler_params=pltpu.CompilerParams(collective_id=0, has_side_effects=True),
     )(spectra.reshape(2, VS_BLK, channels // VS_BLK, bins), channel_mask,

time: 28.6 us -> 26.8 us (0.937)
  Pallas kernels: 27 us -> 25.2 us
    pallas_call x1, Pallas kernels: 27 us -> 25.2 us  [per_device(): pl.pallas_call(functools.partial(kernel, n, nsub, nfrq, chunks, pair_bloc...]
where the time goes in v3:
time: 26.8 us; the launch traced here: 26.6 us
  Pallas kernels  25.2 us (94%)
  local copies, waits for them, and re-layouts  1.38 us (5%)
    pallas_call x1, Pallas kernels, per_device(): pl.pallas_call(functools.partial(kernel, n, nsub, nfrq, chunks, pair_bloc...  25.2 us
    unnamed x1, local copies, waits for them, and re-layouts  1.38 us

profile of v3, /device:TPU:0, one launch (start us, length us, event | category | flops | bytes accessed | tf_op | source)
XLA Modules:
  0.0 26.6 jit_solution(13952133734407358033)
XLA Ops:
  0.0 25.2 %shard_map.82 = f32[32,256]{1,0:T(8,128)} custom-call(bf16[2,32,32,1024]{3,2,1,0:T(8,128)(2,1)} %bitcast.2, s32[1,1024]{1,0:T(1,128)} %mask_ref.1, s32[1,4,48]{2,1,0:T(4,128)} %local_ref.1, s32[1,4,48]{2,1,0:T(4,128)} %partner_ref.1, s32[4,1,48]{2,1,0:T(1,128)} %bitcast.3, s32[1,4,48]{2,1,0:T(4,128)} %slot_ref.1, f32[2,128,1024]{2,1,0:T(8,128)} %constant.4.clone.coarse, ...), custom_call_target="tpu_custom_call" | custom-call | tf_op jit(solution)/shard_map/pallas_call | solution.py:365
  25.2 1.4 %copy.10 = f32[32,256]{1,0:T(8,128)} copy(f32[32,256]{1,0:T(8,128)} %shard_map.82) | data formatting | bytes 65536

commit v4 on v3

--- a/solution.py
+++ b/solution.py
@@ -39,11 +39,12 @@
 
 
 def kernel(n, nsub, nfrq, chunks, pair_block, stack_block,
-           spectra, mask_ref, local_ref, partner_ref, owner_ref, slot_ref, coarse, fine_ref, out_ref,
+           spectra, mask_hbm, local_hbm, partner_hbm, owner_hbm, slot_hbm, coarse, fine_hbm, out_ref,
+           mask_ref, local_ref, partner_ref, owner_ref, slot_ref, fine_ref,
            index_rows, index_cols, stack_row,
            spec, tiles, panels, own, hot, sel, cross, stacked, table, coarse_v, acc,
            send1, recv1, total, send2, recv2,
-           tile_sem, load_sem, right_send, right_recv, left_send, left_recv,
+           list_sem, tile_sem, load_sem, right_send, right_recv, left_send, left_recv,
            s1_send, s1_recv, s2_send, s2_recv):
     z = lax.axis_index("blk")
     sub, frq = lax.axis_index("sub"), lax.axis_index("frq")
@@ -51,16 +52,40 @@
     channels, bins = spec.shape[1], spec.shape[2]
     width = bins // chunks
     pairs, stacks = own.shape[1], acc.shape[0]
-    lag_width = out_ref.shape[1]
+    lag_width = out_ref.shape[2]
     coarse_rows = bins // STEP
     peers = [(ds, df) for ds in range(nsub - 1, -1, -1) for df in range(nfrq - 1, -1, -1)]
 
+    barrier = pltpu.get_barrier_semaphore()
+
+    @pl.when(z + 1 < n)
+    def _():
+        pl.semaphore_signal(barrier, inc=1, device_id={"blk": z + 1}, device_id_type=MESH)
+
+    @pl.when(z - 1 >= 0)
+    def _():
+        pl.semaphore_signal(barrier, inc=1, device_id={"blk": z - 1}, device_id_type=MESH)
+
+    for ds, df in peers[:-1]:
+        pl.semaphore_signal(
+            barrier, inc=1,
+            device_id={"sub": lax.rem(sub + ds, nsub), "frq": lax.rem(frq + df, nfrq)},
+            device_id_type=MESH)
+
+    list_loads = [
+        pltpu.make_async_copy(far, near, list_sem.at[i])
+        for i, (far, near) in enumerate([
+            (mask_hbm, mask_ref), (local_hbm, local_ref), (partner_hbm, partner_ref),
+            (owner_hbm, owner_ref), (slot_hbm, slot_ref), (fine_hbm, fine_ref)])]
+    list_loads[0].start()
     tile_loads = []
     for c in range(chunks):
         lanes = pl.ds(c * width, width)
         tile_loads.append(pltpu.make_async_copy(
             spectra.at[:, :, pl.ds(0, 8), lanes], tiles.at[:, :, :, lanes], tile_sem.at[c]))
     for load in tile_loads:
+        load.start()
+    for load in list_loads[1:5]:
         load.start()
     flat = spectra.reshape(2, channels, bins)
     spec_loads = []
@@ -71,22 +96,7 @@
     coarse_load = pltpu.make_async_copy(
         coarse.at[:, pl.ds(pl.multiple_of(place * coarse_rows, 8), coarse_rows), :],
         coarse_v, load_sem.at[0])
-    barrier = pltpu.get_barrier_semaphore()
-
-    @pl.when(z + 1 < n)
-    def _():
-        pl.semaphore_signal(barrier, inc=1, device_id={"blk": z + 1}, device_id_type=MESH)
-
-    @pl.when(z - 1 >= 0)
-    def _():
-        pl.semaphore_signal(barrier, inc=1, device_id={"blk": z - 1}, device_id_type=MESH)
-
-    for ds, df in peers[:-1]:
-        pl.semaphore_signal(
-            barrier, inc=1,
-            device_id={"sub": lax.rem(sub + ds, nsub), "frq": lax.rem(frq + df, nfrq)},
-            device_id_type=MESH)
-
+    list_loads[0].wait()
     mask = mask_ref[...]
     at_row = lax.broadcasted_iota(jnp.int32, (VS_BLK, channels), 0)
     at_lane = lax.broadcasted_iota(jnp.int32, (VS_BLK, channels), 1)
@@ -155,8 +165,11 @@
     for load in spec_loads:
         load.start()
     coarse_load.start()
+    list_loads[5].start()
 
     def build_hot():
+        for load in list_loads[1:5]:
+            load.wait()
         per_panel = local_ref.shape[2]
         index_rows[...] = jnp.zeros_like(index_rows)
         index_rows[0:n, 0:per_panel] = local_ref[0].astype(jnp.float32)
@@ -197,6 +210,7 @@
     def make_table(c):
         if c == 0:
             coarse_load.wait()
+            list_loads[5].wait()
 
         def body(a):
             row = pl.ds(c * (width // STEP) + a, 1)
@@ -332,16 +346,21 @@
         for k in range(len(peers) - 1):
             share_copy(k, j).wait_send()
     steps(n, shares_left)
-    out_ref[...] = result
-
-    def add_block(k):
+    out_ref[0] = result
+
+    def add_block(keep, k):
         source = lax.rem(z + 1 + k, n)
         pltpu.make_async_remote_copy(
             src_ref=send2.at[source], dst_ref=recv2.at[source],
             send_sem=s2_send.at[source], recv_sem=s2_recv.at[source],
             device_id={"blk": source}, device_id_type=MESH).wait_recv()
-        out_ref[...] += recv2[source].astype(jnp.float32)
-    steps(n - 1, add_block)
+        term = recv2[source].astype(jnp.float32)
+        if keep:
+            out_ref[1] = term
+        else:
+            out_ref[0] += term
+    steps(n - 2, functools.partial(add_block, False))
+    add_block(True, n - 2)
     steps(n - 1, lambda k: owner_copy(lax.rem(z + 1 + k, n)).wait_send())
 
 
@@ -362,12 +381,18 @@
     hbm = pl.BlockSpec(memory_space=pl.ANY)
     peers = nsub * nfrq
     dma = pltpu.SemaphoreType.DMA
-    return pl.pallas_call(
+    halves = pl.pallas_call(
         functools.partial(kernel, n, nsub, nfrq, chunks, pair_block, stack_block),
-        out_shape=jax.ShapeDtypeStruct((SLOTS_DEV, lag_width), f32),
-        in_specs=[hbm, vmem, vmem, vmem, vmem, vmem, hbm, vmem],
+        out_shape=jax.ShapeDtypeStruct((2, SLOTS_DEV, lag_width), f32),
+        in_specs=[hbm] * 8,
         out_specs=vmem,
         scratch_shapes=[
+            pltpu.VMEM(channel_mask.shape, jnp.int32),
+            pltpu.VMEM(local_channel.shape, jnp.int32),
+            pltpu.VMEM(partner_channel.shape, jnp.int32),
+            pltpu.VMEM((n, 1, local_channel.shape[2]), jnp.int32),
+            pltpu.VMEM(stack_slot.shape, jnp.int32),
+            pltpu.VMEM((2, STEP, LAGS), f32),
             pltpu.VMEM((128, 128), f32),
             pltpu.VMEM((pairs, 2), jnp.int32),
             pltpu.VMEM((1, pairs), jnp.int32),
@@ -387,7 +412,7 @@
             pltpu.VMEM((stacks, lag_width), f32),
             pltpu.VMEM((n, SLOTS_DEV, lag_width), bf16),
             pltpu.VMEM((n, SLOTS_DEV, lag_width), bf16),
-            dma((chunks,)), dma((1 + chunks,)),
+            dma((6,)), dma((chunks,)), dma((1 + chunks,)),
             dma((chunks, n - 1)), dma((chunks, n - 1)),
             dma((chunks, n - 1)), dma((chunks, n - 1)),
             dma((peers - 1, n)), dma((peers - 1, n)),
@@ -397,6 +422,7 @@
     )(spectra.reshape(2, VS_BLK, channels // VS_BLK, bins), channel_mask,
       local_channel, partner_channel, stack_owner.reshape(n, 1, -1), stack_slot,
       jnp.asarray(coarse), jnp.asarray(fine))
+    return halves[0] + halves[1]
 
 
 def solution(mesh):

time: 26.8 us -> 25.8 us (0.963)
  other arithmetic: 0 us -> 1.39 us
  local copies, waits for them, and re-layouts: 1.38 us -> 0 us
  Pallas kernels: 25.2 us -> 24.2 us
    add x0 -> x1, other arithmetic: none -> 1.39 us  [per_device(): return halves[0] + halves[1]]
    unnamed x1 -> x0, local copies, waits for them, and re-layouts: 1.38 us -> none
    pallas_call x1, Pallas kernels: 25.2 us -> 24.2 us  [per_device(): pl.pallas_call(functools.partial(kernel, n, nsub, nfrq, chunks, pair_bloc...]
where the time goes in v4:
time: 25.8 us; the launch traced here: 25.7 us
  Pallas kernels  24.2 us (94%)
  other arithmetic  1.39 us (5%)
    pallas_call x1, Pallas kernels, per_device(): pl.pallas_call(functools.partial(kernel, n, nsub, nfrq, chunks, pair_bloc...  24.2 us
    add x1, other arithmetic, per_device(): return halves[0] + halves[1]  1.39 us

profile of v4, /device:TPU:0, one launch (start us, length us, event | category | flops | bytes accessed | tf_op | source)
XLA Modules:
  0.0 25.7 jit_solution(13012910012602362538)
XLA Ops:
  0.0 24.2 %shard_map.82 = f32[2,32,256]{2,1,0:T(8,128)} custom-call(bf16[2,32,32,1024]{3,2,1,0:T(8,128)(2,1)} %bitcast.4, s32[1,1024]{1,0:T(1,128)} %mask_hbm.1, s32[1,4,48]{2,1,0:T(4,128)} %local_hbm.1, s32[1,4,48]{2,1,0:T(4,128)} %partner_hbm.1, s32[4,1,48]{2,1,0:T(1,128)} %bitcast.5, s32[1,4,48]{2,1,0:T(4,128)} %slot_hbm.1, f32[2,128,1024]{2,1,0:T(8,128)} %constant.4.clone.coarse, ...), custom_call_target="tpu_custom_call" | custom-call | tf_op jit(solution)/shard_map/pallas_call | solution.py:384
  24.3 1.4 %add_bitcast_fusion = f32[32,256]{1,0:T(8,128)} fusion(f32[2,32,256]{2,1,0:T(8,128)} %shard_map.82), kind=kLoop, calls=%fused_computation | loop fusion | flops 8192 | bytes 98304 | tf_op jit(solution)/shard_map/add | solution.py:425
